TPU v7x, 256 devices: a whole 4x4x8 slice. The times are simulated.
256 devices in a mesh: req: 64 (over z, y, core), head: 4 (over x).
Axes of the slice: x: 4, y: 4, z: 8, core: 2. Of those that a mesh axis runs over, the one named last changes fastest.
Arguments:
- residual: bfloat16 [1024, 2048], P('req'), may hold values from -5.2 to 5.2
- queries: bfloat16 [1024, 1024], P('req', 'head'), may hold values from -5.5 to 5.5
- new_kv: bfloat16 [1024, 2, 1024], P('req', None, 'head'), may hold values from -4.5 to 4.5
- kv_cache: bfloat16 [8192, 2, 32, 1024], P('req', None, None, 'head'), may hold values from -131 to 131
- lengths: int32 [1024], replicated, may hold values from 2 to 16384, as said below
- slot_request: int32 [8192], P('req'), may hold values from 0 to 1023, as said below
- slot_page: int32 [8192], P('req'), may hold values from 0 to 511, as said below
- slot_used: int32 [8192], P('req'), may hold values from 0 to 1
- out_weight: bfloat16 [1024, 2048], P('head'), may hold values from -0.1875 to 0.1875
- norm_gain: float32 [2048], replicated, may hold values from 0.25 to 1.75
- routes: int32 [1024, 8], P('req'), may hold values from 0 to 63, all different within a row; in each aligned block of 16 rows (0 to 15, 16 to 31, ...) at most 4 rows name the same one
- route_weights: float32 [1024, 8], P('req'), may hold values from 0.05 to 0.5
- w_gate: bfloat16 [64, 2048, 1024], P('req', None, 'head'), may hold values from -0.125 to 0.125
- w_up: bfloat16 [64, 2048, 1024], P('req', None, 'head'), may hold values from -0.125 to 0.125
- w_down: bfloat16 [64, 1024, 2048], P('req', 'head'), may hold values from -0.1875 to 0.1875
- next_gain: float32 [2048], replicated, may hold values from 0.25 to 1.75
- next_weight: bfloat16 [2048, 3, 1024], P(None, None, 'head'), may hold values from -0.125 to 0.125
Outputs:
- stream: bfloat16 [1024, 2048], P('req', 'head')
- next_qkv: bfloat16 [1024, 3, 1024], P('req', None, 'head')
Inputs may be any that keep to these rules, and one draw needn't show every extreme that they name: Request r has cached positions 0 to lengths[r] - 1, held in pages 0 to ceil(lengths[r] / 32) - 1; some request is 16384 long. `slot_request`: each page of every request lies in exactly one slot with slot_used 1; unused slots hold request 0. `slot_page`: unused slots hold page 0. `routes`: within the rows of one index of req at most 4 rows name the same expert.
All inputs are finite; a program needn't handle non-finite values.
Results may differ from a plain program's by a relative error of at most 0.025.
Values may be sent and summed in bfloat16 or wider, within the bound.
No kernel may reach another device: no remote copies, remote signals or barrier semaphores. Data moves between devices by JAX's collectives and lax.ppermute only.
A program may use at most 64 MiB of HBM per device.

v0:
```python
import math
import jax
import jax.numpy as jnp
from jax import lax
from jax.sharding import PartitionSpec as P

HD = 128
EXP_DEV = 1
norm_eps = 1e-06
floor_value = -1e30


def norm_whole(rows_in, gain):
    wide_rows = rows_in.astype(jnp.float32)
    mean_square = jnp.mean(wide_rows * wide_rows, axis=1, keepdims=True)
    return (wide_rows * lax.rsqrt(mean_square + norm_eps) * gain).astype(jnp.bfloat16)


def route_tables(routes, route_weights, expert_total, capacity):
    row_count, pick_count = routes.shape
    flat_routes = routes.reshape(row_count * pick_count)
    hit_table = (flat_routes[:, None] == jnp.arange(expert_total, dtype=jnp.int32)[None, :]).astype(
        jnp.int32
    )
    before = jnp.cumsum(hit_table, axis=0) - hit_table
    slot_rank = jnp.sum(before * hit_table, axis=1)
    target = flat_routes * capacity + slot_rank
    lookup = (
        target[:, None] == jnp.arange(expert_total * capacity, dtype=jnp.int32)[None, :]
    ).astype(jnp.float32)
    lookup = lookup.reshape(row_count, pick_count, expert_total * capacity)
    pick_map = jnp.sum(lookup, axis=1)
    blend_map = jnp.sum(lookup * route_weights[:, :, None], axis=1)
    return (pick_map, blend_map)


def expert_block(arrived, w_gate, w_up, w_down):
    gate_out = jnp.einsum("secd,edf->secf", arrived, w_gate, preferred_element_type=jnp.float32)
    upward = jnp.einsum("secd,edf->secf", arrived, w_up, preferred_element_type=jnp.float32)
    inner_act = (jax.nn.silu(gate_out) * upward).astype(jnp.bfloat16)
    return jnp.einsum("secf,efd->secd", inner_act, w_down, preferred_element_type=jnp.float32)


def local(
    residual,
    queries,
    new_kv,
    kv_cache,
    lengths,
    slot_request,
    slot_page,
    slot_used,
    out_weight,
    norm_gain,
    routes,
    route_weights,
    w_gate,
    w_up,
    w_down,
    next_gain,
    next_weight,
):
    req_rows, row_width = queries.shape
    head_count = row_width // HD
    slot_count = kv_cache.shape[0]
    page_len = kv_cache.shape[2]
    model_width = residual.shape[1]
    req_count = lax.axis_size("req")
    head_total = lax.axis_size("head")
    score_scale = 1.0 / math.sqrt(HD)
    first_row = lax.axis_index("req") * req_rows
    everyone = lax.all_gather(queries, "req", axis=0, tiled=True)
    total_req = everyone.shape[0]
    chosen = everyone[slot_request].reshape(slot_count, head_count, HD)
    key_rows = kv_cache[:, 0].reshape(slot_count, page_len, head_count, HD)
    value_rows = kv_cache[:, 1].reshape(slot_count, page_len, head_count, HD)
    scores = (
        jnp.einsum("sphd,shd->sph", key_rows, chosen, preferred_element_type=jnp.float32)
        * score_scale
    )
    position = slot_page[:, None] * page_len + jnp.arange(page_len, dtype=jnp.int32)[None, :]
    valid = (slot_used[:, None] == 1) & (position < lengths[slot_request][:, None])
    masked = jnp.where(valid[:, :, None], scores, floor_value)
    slot_peak = jnp.max(masked, axis=1)
    member = slot_request[None, :] == jnp.arange(total_req, dtype=jnp.int32)[:, None]
    local_peak = jnp.max(jnp.where(member[:, :, None], slot_peak[None], floor_value), axis=1)
    fresh_key = new_kv[:, 0].reshape(req_rows, head_count, HD)
    fresh_value = new_kv[:, 1].astype(jnp.float32).reshape(req_rows, head_count, HD)
    own_query = queries.reshape(req_rows, head_count, HD)
    own_score = (
        jnp.einsum("rhd,rhd->rh", own_query, fresh_key, preferred_element_type=jnp.float32)
        * score_scale
    )
    placed_score = lax.dynamic_update_slice(
        jnp.full((total_req, head_count), floor_value, jnp.float32), own_score, (first_row, 0)
    )
    peak_score = lax.pmax(jnp.maximum(local_peak, placed_score), "req")
    weights = jnp.where(
        valid[:, :, None], jnp.exp(masked - peak_score[slot_request][:, None, :]), 0.0
    ).astype(jnp.bfloat16)
    slot_numer = jnp.einsum(
        "sph,sphd->shd", weights, value_rows, preferred_element_type=jnp.float32
    ).reshape(slot_count, row_width)
    slot_denom = jnp.sum(weights.astype(jnp.float32), axis=1)
    member_float = member.astype(jnp.float32)
    numerator = jnp.dot(member_float, slot_numer, precision=lax.Precision.HIGHEST)
    denominator = jnp.dot(member_float, slot_denom, precision=lax.Precision.HIGHEST)
    numerator, denominator = (
        lax.psum_scatter(numerator, "req", scatter_dimension=0, tiled=True),
        lax.psum_scatter(denominator, "req", scatter_dimension=0, tiled=True),
    )
    own_peak = lax.dynamic_slice_in_dim(peak_score, first_row, req_rows, 0)
    new_lift = jnp.exp(own_score - own_peak)
    mixed_rows = (
        numerator.reshape(req_rows, head_count, HD) + new_lift[:, :, None] * fresh_value
    ) / (denominator + new_lift)[:, :, None]
    attended = mixed_rows.reshape(req_rows, row_width).astype(jnp.bfloat16)
    partial_out = jnp.dot(attended, out_weight, preferred_element_type=jnp.float32)
    expert_total = EXP_DEV * req_count
    pick_count = routes.shape[1]
    capacity = min(
        req_rows, max(2, 2 * ((req_rows * pick_count + expert_total - 1) // expert_total))
    )
    slot_cells = expert_total * capacity
    pick_map, blend_map = route_tables(routes, route_weights, expert_total, capacity)
    pick_bf = pick_map.astype(jnp.bfloat16)
    slice_width = model_width // head_total
    first_col = lax.axis_index("head") * slice_width
    attn_out = lax.psum(partial_out.astype(jnp.bfloat16), "head").astype(jnp.float32)
    hidden_state = (residual.astype(jnp.float32) + attn_out).astype(jnp.bfloat16)
    normed = norm_whole(hidden_state, norm_gain)
    buffer = jnp.einsum("rc,rd->cd", pick_bf, normed, preferred_element_type=jnp.float32).astype(
        jnp.bfloat16
    )
    buffer = buffer.reshape(req_count, EXP_DEV, capacity, model_width)
    expert_part = expert_block(
        lax.all_to_all(buffer, "req", split_axis=0, concat_axis=0, tiled=True), w_gate, w_up, w_down
    )
    expert_sum = lax.psum(expert_part.astype(jnp.bfloat16), "head")
    returned = lax.all_to_all(expert_sum, "req", split_axis=0, concat_axis=0, tiled=True)
    moe_sum = jnp.dot(
        blend_map,
        returned.reshape(slot_cells, model_width).astype(jnp.float32),
        precision=lax.Precision.HIGHEST,
    )
    stream_full = (hidden_state.astype(jnp.float32) + moe_sum).astype(jnp.bfloat16)
    next_normed = norm_whole(stream_full, next_gain)
    stream_out = lax.dynamic_slice_in_dim(stream_full, first_col, slice_width, 1)
    next_qkv = jnp.einsum(
        "td,dcf->tcf", next_normed, next_weight, preferred_element_type=jnp.float32
    ).astype(jnp.bfloat16)
    return (stream_out, next_qkv)


def solution(mesh):
    placed = (
        P("req", None),
        P("req", "head"),
        P("req", None, "head"),
        P("req", None, None, "head"),
        P(),
        P("req"),
        P("req"),
        P("req"),
        P("head", None),
        P(),
        P("req", None),
        P("req", None),
        P("req", None, "head"),
        P("req", None, "head"),
        P("req", "head", None),
        P(),
        P(None, None, "head"),
    )
    return jax.shard_map(
        local,
        mesh=mesh,
        in_specs=placed,
        out_specs=(P("req", "head"), P("req", None, "head")),
        check_vma=False,
    )
```

profile of v0, /device:TPU:1, one launch (start us, length us, event | category | flops | bytes accessed | tf_op | source)
XLA Modules:
  0.0 685.3 jit_solution(6370104238343383896)
XLA Ops:
  8.0 0.8 iota_compare_fusion
  8.9 59.8 %all_gather.3 = bf16[1024,256]{1,0:T(8,128)(2,1)} all-gather(bf16[16,256]{1,0:T(8,128)(2,1)} %param.18), channel_id=1, replica_groups=mesh['req'=64,'head'=4] {'req'}, dimensions={0}, use_global_device_ids=true | all-gather | bytes 532480 | tf_op jit(solution)/shard_map/all_gather | solution.py:72
  69.4 1.9 gather_fusion.1
  71.9 4.6 fusion.59
  76.5 4.0 reshape_squeeze.9
  80.5 2.9 fusion.4
  83.5 1.0 gather_fusion
  84.9 1.0 copy.43
  86.2 1.9 max.5
  88.1 247.3 %pmax.7 = f32[1024,2]{1,0:T(8,128)} all-reduce(f32[1024,2]{1,0:T(8,128)} %max.5), channel_id=1, replica_groups=mesh['req'=64,'head'=4] {'req'}, use_global_device_ids=true, to_apply=%region_2.3 | all-reduce | flops 2048 | bytes 16384 | tf_op jit(solution)/shard_map/pmax | solution.py:97
  335.4 1.7 gather_fusion.2
  337.3 4.0 reshape_squeeze.11
  341.3 2.3 fusion.2
  343.6 1.6 fusion.21
  347.7 131.2 %all-reduce = f32[1024,2]{0,1:T(2,128)S(1)} all-reduce(f32[1024,2]{0,1:T(2,128)S(1)} %fusion.20), channel_id=3, replica_groups=mesh['req'=64,'head'=4] {'req'}, use_global_device_ids=true, to_apply=%region_5.6.clone | all-reduce | flops 2048 | bytes 16384
  479.7 1.4 reduce-scatter.3.cloned.1.call-done
  481.3 2.1 convolution_convert_fusion.2
  483.7 47.1 %all-reduce.4.cloned.1.call-done = bf16[16,2048]{1,0:T(8,128)(2,1)} async-done(((bf16[16,2048]{1,0:T(8,128)(2,1)}), bf16[16,2048]{1,0:T(8,128)(2,1)}) %all-reduce.4.cloned.1.call-update) | async-done | bytes 65552 | tf_op jit(solution)/shard_map/psum | solution.py:129
  530.8 1.0 fusion.32
  531.8 2.3 convolution_convert_fusion.1
  534.1 2.3 reshape.165
  536.3 40.8 %all_to_all.10 = bf16[64,1,4,2048]{3,2,1,0:T(4,128)(2,1)S(1)} all-to-all(bf16[64,1,4,2048]{3,2,1,0:T(4,128)(2,1)} %bitcast.123), channel_id=1, replica_groups=mesh['req'=64,'head'=4] {'req'}, dimensions={0} | all-to-all | bytes 2097152 | tf_op jit(solution)/shard_map/all_to_all | solution.py:137
  577.2 1.0 copy-done.2
  578.1 1.3 convolution_bitcast_fusion.1
  579.4 4.2 fusion
  583.7 45.9 %all-reduce.6.cloned.1.call-done = bf16[64,1,4,2048]{3,0,2,1:T(8,128)(2,1)} async-done(((bf16[64,1,4,2048]{3,0,2,1:T(8,128)(2,1)}), bf16[64,1,4,2048]{3,0,2,1:T(8,128)(2,1)}) %all-reduce.6.cloned.1.call-update) | async-done | bytes 1048592 | tf_op jit(solution)/shard_map/psum | solution.py:139
  629.5 3.1 copy.52
  632.6 12.4 %all-to-all-start.1 = ((bf16[64,1,4,2048]{3,2,1,0:T(4,128)(2,1)}), bf16[64,1,4,2048]{3,2,1,0:T(4,128)(2,1)}, u32[]{:S(2)}, u32[]{:S(2)}) async-start(bf16[64,1,4,2048]{3,2,1,0:T(4,128)(2,1)} %copy.52), calls=%async_computation.2 | async-start | bytes 2097152 | tf_op jit(solution)/shard_map/all_to_all | solution.py:140
  645.0 27.9 %all-to-all-done.1 = bf16[64,1,4,2048]{3,2,1,0:T(4,128)(2,1)} async-done(((bf16[64,1,4,2048]{3,2,1,0:T(4,128)(2,1)}), bf16[64,1,4,2048]{3,2,1,0:T(4,128)(2,1)}, u32[]{:S(2)}, u32[]{:S(2)}) %all-to-all-start.1) | async-done | bytes 1048608 | tf_op jit(solution)/shard_map/all_to_all | solution.py:140
  672.9 2.2 reshape.171
  675.1 1.9 fusion.29
  677.6 1.2 convolution_convert_fusion.3
  (72 shorter events, 6.9 us)
Async XLA Ops:
  7.2 670.4 %copy-start = (bf16[2048,3,256]{2,0,1:T(8,128)(2,1)S(1)}, bf16[2048,3,256]{2,0,1:T(8,128)(2,1)}, u32[]{:S(2)}) copy-start(bf16[2048,3,256]{2,0,1:T(8,128)(2,1)} %param.33) | copy-start | bytes 9437188
  7.2 474.0 %reduce-scatter.3.cloned.1.call-start = ((), (), s32[]{:S(2)}) async-start(), calls=%async_computation.3 | async-start | bytes 1064960 | tf_op jit(solution)/shard_map/reduce_scatter | solution.py:109
  80.5 3.0 copy-start.1
  80.5 4.0 copy-start.12
  80.5 4.0 copy-start.13
  80.5 5.5 copy-start.5
  341.3 2.3 copy-start.10
  341.3 4.0 copy-start.8
  341.3 4.7 copy-start.9
  341.3 4.8 copy-start.14
  343.6 187.2 %copy-start.3 = (bf16[16,2048]{1,0:T(8,128)(2,1)S(1)}, bf16[16,2048]{1,0:T(8,128)(2,1)}, u32[]{:S(2)}) copy-start(bf16[16,2048]{1,0:T(8,128)(2,1)} %param.17) | copy-start | bytes 196612
  343.6 188.1 %copy-start.6 = (f32[2048]{0:T(1024)S(1)}, f32[2048]{0:T(1024)}, u32[]{:S(2)}) copy-start(f32[2048]{0:T(1024)} %param.26) | copy-start | bytes 24580
  345.2 185.5 %all-reduce.4.cloned.1.call-start = ((), (), s32[]{:S(2)}) async-start(), calls=%async_computation.4 | async-start | bytes 131072 | tf_op jit(solution)/shard_map/psum | solution.py:129
  483.5 146.1 %all-reduce.6.cloned.1.call-start = ((), (), s32[]{:S(2)}) async-start(), calls=%async_computation.5 | async-start | bytes 2097152 | tf_op jit(solution)/shard_map/psum | solution.py:139
  536.3 41.8 %copy-start.11 = (bf16[1,2048,256]{2,1,0:T(8,128)(2,1)S(1)}, bf16[1,2048,256]{2,1,0:T(8,128)(2,1)}, u32[]{:S(2)}) copy-start(bf16[1,2048,256]{2,1,0:T(8,128)(2,1)} %param.29) | copy-start | bytes 3145732
  577.2 1.0 copy-start.2
  632.6 42.5 %copy-start.4 = (bf16[16,2048]{1,0:T(8,128)(2,1)S(1)}, bf16[16,2048]{1,0:T(8,128)(2,1)}, u32[]{:S(2)}) copy-start(bf16[16,2048]{1,0:T(8,128)(2,1)} %all-reduce.4.cloned.1.call-done) | copy-start | bytes 196612
  632.6 40.3 %all-to-all-start.1 = ((bf16[64,1,4,2048]{3,2,1,0:T(4,128)(2,1)}), bf16[64,1,4,2048]{3,2,1,0:T(4,128)(2,1)}, u32[]{:S(2)}, u32[]{:S(2)}) async-start(bf16[64,1,4,2048]{3,2,1,0:T(4,128)(2,1)} %copy.52), calls=%async_computation.2 | async-start | bytes 2097152 | tf_op jit(solution)/shard_map/all_to_all | solution.py:140
  645.0 32.6 %copy-start.7 = (f32[2048]{0:T(1024)S(1)}, f32[2048]{0:T(1024)}, u32[]{:S(2)}) copy-start(f32[2048]{0:T(1024)} %param.32) | copy-start | bytes 24580
Sparse Core Ops, SparseCore 0:
  345.4 135.7 reduce-scatter.2
  483.6 47.1 all-reduce.3
  583.8 45.6 all-reduce.5
where the time goes:
time: 686 us; the launch traced here: 685 us
  blocking collectives  479 us (70%)
  waiting for transfers between devices  122 us (18%)
  local copies, waits for them, and re-layouts  30.3 us (4%)
  matrix products  20 us (3%)
  between operations  14.6 us (2%)
  starting transfers between devices  12.5 us (2%)
    pmax x1, blocking collectives, local(): peak_score = lax.pmax(jnp.maximum(local_peak, placed_score), 'req')  247 us
    unnamed x1, blocking collectives  131 us
    all_gather x1, blocking collectives, local(): everyone = lax.all_gather(queries, 'req', axis=0, tiled=True)  59.8 us
    psum x1, waiting for transfers between devices, local(): lax.psum(partial_out.astype(jnp.bfloat16), 'head').astype(jnp.float32)  47.1 us
    psum x1, waiting for transfers between devices, local(): expert_sum = lax.psum(expert_part.astype(jnp.bfloat16), 'head')  45.9 us
    all_to_all x1, blocking collectives, local(): lax.all_to_all(buffer, 'req', split_axis=0, concat_axis=0, tiled=True)  40.8 us
    all_to_all x1, waiting for transfers between devices, local(): lax.all_to_all(expert_sum, 'req', split_axis=0, concat_axis=0, tiled=True)  27.9 us
  transfers between devices with their start and end apart: 4, of which 4 were waited for; matrix products, arithmetic and copies ran while one was open for 0% of the time, Pallas kernels for 0%

commit v1 on v0

--- a/solution.py
+++ b/solution.py
@@ -69,7 +69,9 @@
     head_total = lax.axis_size("head")
     score_scale = 1.0 / math.sqrt(HD)
     first_row = lax.axis_index("req") * req_rows
-    everyone = lax.all_gather(queries, "req", axis=0, tiled=True)
+    everyone = jnp.concatenate(
+        lax.all_to_all(jnp.stack([queries] * lax.axis_size("req")), "req", 0, 0), axis=0
+    )
     total_req = everyone.shape[0]
     chosen = everyone[slot_request].reshape(slot_count, head_count, HD)
     key_rows = kv_cache[:, 0].reshape(slot_count, page_len, head_count, HD)

time: 686 us -> 644 us (0.939)
  blocking collectives: 479 us -> 420 us
  starting transfers between devices: 12.5 us -> 25.9 us
    all_gather x1 -> x0, blocking collectives: 59.8 us -> none  [local(): everyone = lax.all_gather(queries, 'req', axis=0, tiled=True)]
    all_to_all x0 -> x1, starting transfers between devices: none -> 13.3 us  [local(): lax.all_to_all(jnp.stack([queries] * lax.axis_size('req')), 'req', 0, 0)]
  transfers between devices with their start and end apart: 4 -> 5, of which waited for: 4 -> 5; matrix products, arithmetic and copies ran while one was open for 0% -> 3% of each run, Pallas kernels for 0% -> 0%
where the time goes in v1:
time: 644 us; the launch traced here: 643 us
  blocking collectives  420 us (65%)
  waiting for transfers between devices  124 us (19%)
  local copies, waits for them, and re-layouts  32.2 us (5%)
  starting transfers between devices  25.9 us (4%)
  matrix products  19.9 us (3%)
  between operations  14.7 us (2%)
    pmax x1, blocking collectives, local(): peak_score = lax.pmax(jnp.maximum(local_peak, placed_score), 'req')  248 us
    unnamed x1, blocking collectives  131 us
    psum x1, waiting for transfers between devices, local(): lax.psum(partial_out.astype(jnp.bfloat16), 'head').astype(jnp.float32)  47.1 us
    psum x1, waiting for transfers between devices, local(): expert_sum = lax.psum(expert_part.astype(jnp.bfloat16), 'head')  45.9 us
    all_to_all x1, blocking collectives, local(): lax.all_to_all(buffer, 'req', split_axis=0, concat_axis=0, tiled=True)  40.8 us
    all_to_all x1, waiting for transfers between devices, local(): lax.all_to_all(expert_sum, 'req', split_axis=0, concat_axis=0, tiled=True)  27.9 us
    all_to_all x1, starting transfers between devices, local(): lax.all_to_all(jnp.stack([queries] * lax.axis_size('req')), 'req', 0, 0)  13.3 us
  transfers between devices with their start and end apart: 5, of which 5 were waited for; matrix products, arithmetic and copies ran while one was open for 3% of the time, Pallas kernels for 0%

profile of v1, /device:TPU:1, one launch (start us, length us, event | category | flops | bytes accessed | tf_op | source)
XLA Modules:
  0.0 643.1 jit_solution(2674278678109125508)
XLA Ops:
  7.2 1.7 stack.2
  8.9 13.3 %all-to-all-start = ((bf16[64,16,256]{2,1,0:T(8,128)(2,1)}), bf16[64,16,256]{2,1,0:T(8,128)(2,1)}, u32[]{:S(2)}, u32[]{:S(2)}) async-start(bf16[64,16,256]{2,1,0:T(8,128)(2,1)} %stack.2), calls=%async_computation | async-start | bytes 1048576 | tf_op jit(solution)/shard_map/all_to_all | solution.py:73
  23.0 4.7 fusion.59
  27.8 4.0 reshape_squeeze.9
  31.8 4.0 reshape_squeeze.11
  38.4 1.5 all-to-all-done
  39.9 1.9 gather_fusion.1
  42.4 2.8 fusion.4
  45.7 1.0 copy.43
  46.8 2.1 max.5
  48.8 248.4 %pmax.7 = f32[1024,2]{1,0:T(8,128)} all-reduce(f32[1024,2]{1,0:T(8,128)} %max.5), channel_id=1, replica_groups=mesh['req'=64,'head'=4] {'req'}, use_global_device_ids=true, to_apply=%region_2.3 | all-reduce | flops 2048 | bytes 16384 | tf_op jit(solution)/shard_map/pmax | solution.py:99
  297.2 1.7 gather_fusion.2
  299.2 2.2 fusion.2
  301.5 1.6 fusion.21
  305.5 131.3 %all-reduce = f32[1024,2]{0,1:T(2,128)S(1)} all-reduce(f32[1024,2]{0,1:T(2,128)S(1)} %fusion.20), channel_id=3, replica_groups=mesh['req'=64,'head'=4] {'req'}, use_global_device_ids=true, to_apply=%region_5.6.clone | all-reduce | flops 2048 | bytes 16384
  437.7 1.3 reduce-scatter.3.cloned.1.call-done
  439.1 2.1 convolution_convert_fusion.2
  441.5 47.1 %all-reduce.4.cloned.1.call-done = bf16[16,2048]{1,0:T(8,128)(2,1)} async-done(((bf16[16,2048]{1,0:T(8,128)(2,1)}), bf16[16,2048]{1,0:T(8,128)(2,1)}) %all-reduce.4.cloned.1.call-update) | async-done | bytes 65552 | tf_op jit(solution)/shard_map/psum | solution.py:131
  488.6 1.0 fusion.32
  489.5 2.3 convolution_convert_fusion.1
  491.8 2.3 reshape.171
  494.1 40.8 %all_to_all.15 = bf16[64,1,4,2048]{3,2,1,0:T(4,128)(2,1)S(1)} all-to-all(bf16[64,1,4,2048]{3,2,1,0:T(4,128)(2,1)} %bitcast.124), channel_id=1, replica_groups=mesh['req'=64,'head'=4] {'req'}, dimensions={0} | all-to-all | bytes 2097152 | tf_op jit(solution)/shard_map/all_to_all | solution.py:139
  534.9 1.0 copy-done.2
  535.9 1.3 convolution_bitcast_fusion.1
  537.2 4.2 fusion
  541.4 45.9 %all-reduce.6.cloned.1.call-done = bf16[64,1,4,2048]{3,0,2,1:T(8,128)(2,1)} async-done(((bf16[64,1,4,2048]{3,0,2,1:T(8,128)(2,1)}), bf16[64,1,4,2048]{3,0,2,1:T(8,128)(2,1)}) %all-reduce.6.cloned.1.call-update) | async-done | bytes 1048592 | tf_op jit(solution)/shard_map/psum | solution.py:141
  587.3 3.1 copy.52
  590.4 12.4 %all-to-all-start.2 = ((bf16[64,1,4,2048]{3,2,1,0:T(4,128)(2,1)}), bf16[64,1,4,2048]{3,2,1,0:T(4,128)(2,1)}, u32[]{:S(2)}, u32[]{:S(2)}) async-start(bf16[64,1,4,2048]{3,2,1,0:T(4,128)(2,1)} %copy.52), calls=%async_computation.3 | async-start | bytes 2097152 | tf_op jit(solution)/shard_map/all_to_all | solution.py:142
  602.8 27.9 %all-to-all-done.2 = bf16[64,1,4,2048]{3,2,1,0:T(4,128)(2,1)} async-done(((bf16[64,1,4,2048]{3,2,1,0:T(4,128)(2,1)}), bf16[64,1,4,2048]{3,2,1,0:T(4,128)(2,1)}, u32[]{:S(2)}, u32[]{:S(2)}) %all-to-all-start.2) | async-done | bytes 1048608 | tf_op jit(solution)/shard_map/all_to_all | solution.py:142
  630.7 2.2 reshape.177
  632.9 1.9 fusion.29
  635.4 1.2 convolution_convert_fusion.3
  (76 shorter events, 8.5 us)
Async XLA Ops:
  7.2 628.2 %copy-start = (bf16[2048,3,256]{2,0,1:T(8,128)(2,1)S(1)}, bf16[2048,3,256]{2,0,1:T(8,128)(2,1)}, u32[]{:S(2)}) copy-start(bf16[2048,3,256]{2,0,1:T(8,128)(2,1)} %param.33) | copy-start | bytes 9437188
  8.9 31.0 %all-to-all-start = ((bf16[64,16,256]{2,1,0:T(8,128)(2,1)}), bf16[64,16,256]{2,1,0:T(8,128)(2,1)}, u32[]{:S(2)}, u32[]{:S(2)}) async-start(bf16[64,16,256]{2,1,0:T(8,128)(2,1)} %stack.2), calls=%async_computation | async-start | bytes 1048576 | tf_op jit(solution)/shard_map/all_to_all | solution.py:73
  22.2 416.7 %reduce-scatter.3.cloned.1.call-start = ((), (), s32[]{:S(2)}) async-start(), calls=%async_computation.4 | async-start | bytes 1064960 | tf_op jit(solution)/shard_map/reduce_scatter | solution.py:111
  22.9 4.7 copy-start.13
  22.9 4.7 copy-start.5
  22.9 4.8 copy-start.6
  31.8 4.0 copy-start.1
  31.8 5.1 copy-start.14
  31.8 6.5 %copy-start.11 = (s32[128]{0:T(128)S(1)}, s32[128]{0:T(128)}, u32[]{:S(2)}) copy-start(s32[128]{0:T(128)} %param.22) | copy-start | bytes 1540
  299.2 4.0 copy-start.9
  299.2 4.7 copy-start.10
  299.2 4.7 copy-start.15
  301.4 187.1 %copy-start.3 = (bf16[16,2048]{1,0:T(8,128)(2,1)S(1)}, bf16[16,2048]{1,0:T(8,128)(2,1)}, u32[]{:S(2)}) copy-start(bf16[16,2048]{1,0:T(8,128)(2,1)} %param.17) | copy-start | bytes 196612
  301.5 188.1 %copy-start.7 = (f32[2048]{0:T(1024)S(1)}, f32[2048]{0:T(1024)}, u32[]{:S(2)}) copy-start(f32[2048]{0:T(1024)} %param.26) | copy-start | bytes 24580
  303.1 185.5 %all-reduce.4.cloned.1.call-start = ((), (), s32[]{:S(2)}) async-start(), calls=%async_computation.5 | async-start | bytes 131072 | tf_op jit(solution)/shard_map/psum | solution.py:131
  441.3 146.0 %all-reduce.6.cloned.1.call-start = ((), (), s32[]{:S(2)}) async-start(), calls=%async_computation.6 | async-start | bytes 2097152 | tf_op jit(solution)/shard_map/psum | solution.py:141
  494.1 41.8 %copy-start.12 = (bf16[1,2048,256]{2,1,0:T(8,128)(2,1)S(1)}, bf16[1,2048,256]{2,1,0:T(8,128)(2,1)}, u32[]{:S(2)}) copy-start(bf16[1,2048,256]{2,1,0:T(8,128)(2,1)} %param.29) | copy-start | bytes 3145732
  534.9 1.0 copy-start.2
  590.4 42.5 %copy-start.4 = (bf16[16,2048]{1,0:T(8,128)(2,1)S(1)}, bf16[16,2048]{1,0:T(8,128)(2,1)}, u32[]{:S(2)}) copy-start(bf16[16,2048]{1,0:T(8,128)(2,1)} %all-reduce.4.cloned.1.call-done) | copy-start | bytes 196612
  590.4 40.3 %all-to-all-start.2 = ((bf16[64,1,4,2048]{3,2,1,0:T(4,128)(2,1)}), bf16[64,1,4,2048]{3,2,1,0:T(4,128)(2,1)}, u32[]{:S(2)}, u32[]{:S(2)}) async-start(bf16[64,1,4,2048]{3,2,1,0:T(4,128)(2,1)} %copy.52), calls=%async_computation.3 | async-start | bytes 2097152 | tf_op jit(solution)/shard_map/all_to_all | solution.py:142
  602.8 32.6 %copy-start.8 = (f32[2048]{0:T(1024)S(1)}, f32[2048]{0:T(1024)}, u32[]{:S(2)}) copy-start(f32[2048]{0:T(1024)} %param.32) | copy-start | bytes 24580
Sparse Core Ops, SparseCore 0:
  303.2 135.7 reduce-scatter.2
  441.4 47.1 all-reduce.3
  541.6 45.7 all-reduce.5
